TPU v7x, 32 devices: a whole 2x2x4 slice. The times are simulated.
32 devices in a mesh: plane: 2 (over x), coil: 16 (over z, y, core).
Axes of the slice: x: 2, y: 2, z: 4, core: 2. Of those that a mesh axis runs over, the one named last changes fastest.
Arguments:
- image: float32 [512, 8, 512], P(('plane', 'coil')), parts along dimension 0, may hold values from -6 to 6
- sens: float32 [512, 32, 512], P(('plane', 'coil')), parts along dimension 0, may hold values from -0.75 to 0.75
- kspace: float32 [512, 256, 512], P('plane', 'coil'), parts along dimension 0, may hold values from -6 to 6
- mask: int32 [8, 256], replicated, may hold values 0 or 1
Outputs:
- recon: float32 [512, 8, 512], P(('plane', 'coil')), parts along dimension 0
There are 2 independent parts, one for each index of `plane`. A program takes and returns all parts, laid end to end along the dimension named above; an argument that names none is the same for every part. Nothing has to cross between parts.
Inputs may be any that keep to these rules, and one draw needn't show every extreme that they name: mask[f, ky] is 1 where phase-encode line ky is sampled in frame f, else 0.
All inputs are finite; a program needn't handle non-finite values.
Results may differ from a plain program's by a relative error of at most 0.0001.
Values sent between devices are 32-bit elements; how exact they have to be, the bound alone decides.
A program may use at most 128 MiB of HBM per device.

v0:
```python
import jax
import jax.numpy as jnp
import numpy as np
from jax import lax
from jax.experimental import pallas as pl
from jax.experimental.pallas import tpu as pltpu
from jax.sharding import PartitionSpec as P

OUTER = 2
INNER = 2

step_size = 0.5
tv_weight = 0.1
dual_step = 1.25
high = lax.Precision.HIGH


def contract(spec, *operands):
    return jnp.einsum(spec, *operands, precision=high, preferred_element_type=jnp.float32)


def dft_tables(length):
    index = lax.iota(jnp.int32, length)
    product = index[:, None] * index[None, :] % length
    angle = 2.0 * jnp.pi / length * product.astype(jnp.float32)
    scale = 1.0 / jnp.sqrt(jnp.float32(length))
    return (jnp.cos(angle) * scale, -jnp.sin(angle) * scale)


def column_matrix(cos_part, sin_part):
    upper = jnp.concatenate([cos_part, sin_part], 1)
    lower = jnp.concatenate([-sin_part, cos_part], 1)
    return jnp.concatenate([upper, lower], 0)


def projections(mask, row_cos, row_sin):
    weights = mask.astype(jnp.float32)
    wide = jnp.concatenate([row_cos, row_sin], 1)
    cos_rows = weights[:, :, None] * row_cos[None]
    sin_rows = weights[:, :, None] * row_sin[None]
    from_cos = contract("fka,ky->fay", cos_rows, wide)
    from_sin = contract("fka,ky->fay", sin_rows, wide)
    length = row_cos.shape[0]
    real = from_cos[..., :length] + from_sin[..., length:]
    imag = from_cos[..., length:] - from_sin[..., :length]
    return (real, imag)


def to_columns(field, devices):
    rows, count, packed = field.shape
    width = packed // 2 // devices
    parts = field.reshape(rows, count, 2, devices, width)
    return jnp.transpose(parts, (3, 0, 2, 1, 4)).reshape(devices, rows, 2 * count * width)


def divergence(dual_time, dual_rows):
    time_axis, row_axis = 1, 3
    zero_time = jnp.zeros_like(dual_time[:, :1])
    zero_rows = jnp.zeros_like(dual_rows[..., :1])
    head_time = dual_time[:, :-1]
    head_rows = dual_rows[..., :-1]
    from_time = jnp.concatenate([zero_time, head_time], time_axis) - jnp.concatenate(
        [head_time, zero_time], time_axis
    )
    from_rows = jnp.concatenate([zero_rows, head_rows], row_axis) - jnp.concatenate(
        [head_rows, zero_rows], row_axis
    )
    return from_time + from_rows


def forward_diff(field):
    diff_time = jnp.concatenate(
        [field[:, 1:] - field[:, :-1], jnp.zeros_like(field[:, :1])], 1
    )
    diff_rows = jnp.concatenate(
        [field[..., 1:] - field[..., :-1], jnp.zeros_like(field[..., :1])], 3
    )
    return (diff_time, diff_rows)


def denoise(target):
    dual_time = jnp.zeros_like(target)
    dual_rows = jnp.zeros_like(target)
    for repeat in range(INNER):
        primal = target
        if repeat:
            primal = target - tv_weight * divergence(dual_time, dual_rows)
        diff_time, diff_rows = forward_diff(primal)
        dual_time = jnp.clip(dual_time + dual_step * diff_time, -1.0, 1.0)
        dual_rows = jnp.clip(dual_rows + dual_step * diff_rows, -1.0, 1.0)
    return target - tv_weight * divergence(dual_time, dual_rows)


def iterate(field, data_term, maps, real, imag):
    maps_re, maps_im = (maps[0][None], maps[1][None])
    for sweep in range(OUTER):
        now_re, now_im = (field[0][:, None], field[1][:, None])
        seen_re = maps_re * now_re - maps_im * now_im
        seen_im = maps_re * now_im + maps_im * now_re
        kept_re = contract("fczy,fky->fczk", seen_re, real) - contract(
            "fczy,fky->fczk", seen_im, imag
        )
        kept_im = contract("fczy,fky->fczk", seen_re, imag) + contract(
            "fczy,fky->fczk", seen_im, real
        )
        grad_re = jnp.sum(maps_re * kept_re + maps_im * kept_im, 1)
        grad_im = jnp.sum(maps_re * kept_im - maps_im * kept_re, 1)
        gradient = jnp.stack([grad_re, grad_im]) - data_term
        field = denoise(field - step_size * gradient)
    return field


def data_images(kspace, mask_pairs, row_cos, row_sin, col_cos, col_sin):
    masked = jnp.transpose(mask_pairs)[:, :, None] * kspace
    mid = contract("kpz,zw->kpw", masked, column_matrix(col_cos, -col_sin))
    half = kspace.shape[-1] // 2
    from_cos = contract("ky,kpz->ypz", row_cos, mid)
    from_sin = contract("ky,kpz->ypz", row_sin, mid)
    real = from_cos[..., :half] + from_sin[..., half:]
    imag = from_cos[..., half:] - from_sin[..., :half]
    return (real, imag)


LANES = 128
SUBLANES = 8


def swap_blocks(values, width):
    count = len(values)
    block = lax.broadcasted_iota(jnp.int32, values[0].shape, 1) // width
    step = count // 2
    while step:
        lower = block // step % 2 == 0
        shift = step * width
        values = list(values)
        for at in range(count):
            if at // step % 2 == 0:
                near, far = (values[at], values[at + step])
                values[at] = jnp.where(lower, near, pltpu.roll(far, shift, 1))
                values[at + step] = jnp.where(lower, pltpu.roll(near, LANES - shift, 1), far)
        step //= 2
    return values


def blocked(devices, width, rows, length, half, coils, frames, pairs):
    group = LANES // width
    fits = LANES % width == 0 and width % SUBLANES == 0 and rows % SUBLANES == 0
    fits = fits and devices % group == 0 and coils % group == 0 and frames % group == 0
    fits = fits and devices >= SUBLANES and devices & (devices - 1) == 0
    fits = fits and pairs % frames == 0 and coils * frames == pairs * devices
    return fits and length % (2 * LANES) == 0 and half % LANES == 0


def pack_kernel(devices, width, sens_ref, image_ref, out_ref):
    group = LANES // width
    half = devices * width
    start = 0
    for source in (sens_ref, image_ref):
        count = source.shape[0]
        for part in range(2):
            for tile in range(half // LANES):
                lane = part * half + tile * LANES
                for first in range(0, count, group):
                    taken = [source[first + at, :, lane : lane + LANES] for at in range(group)]
                    target = start + (part * count + first) * width
                    for at, value in enumerate(swap_blocks(taken, width)):
                        out_ref[tile * group + at, :, target : target + LANES] = value
        start += 2 * count * width


def split(value):
    top = value.astype(jnp.bfloat16)
    return (top, (value - top.astype(jnp.float32)).astype(jnp.bfloat16))


def narrow(value):
    value = value.astype(np.float32)
    top = value.astype(jnp.bfloat16)
    return np.stack([top, (value - top.astype(np.float32)).astype(jnp.bfloat16)])


def mix_left(value):
    top, low = split(value)
    return jnp.concatenate([low, top, top], 1)


def mix_right(pair):
    return jnp.concatenate([pair[0], pair[1], pair[0]], 0)


def dot(left, right):
    return jnp.dot(left, right, preferred_element_type=jnp.float32)


def row_tables(length):
    half = length // 2
    tables = []
    for odd in range(2):
        product = np.outer(np.arange(half), 2 * np.arange(half) + odd) % length
        angle = 2.0 * np.pi / length * product
        cos_part, sin_part = (np.cos(angle) / np.sqrt(length), np.sin(angle) / np.sqrt(length))
        tables.append(narrow(np.block([[cos_part, -sin_part], [sin_part, cos_part]])))
    return np.stack(tables)


def column_table(length):
    angle = 2.0 * np.pi / length * (np.outer(np.arange(length), np.arange(length)) % length)
    cos_part, sin_part = (np.cos(angle) / np.sqrt(length), np.sin(angle) / np.sqrt(length))
    return narrow(np.block([[cos_part, sin_part], [-sin_part, cos_part]]))


MESH = pl.DeviceIdType.MESH


def greet(peers):
    barrier = pltpu.get_barrier_semaphore()
    for peer in peers:
        pl.semaphore_signal(barrier, 1, device_id={"coil": peer}, device_id_type=MESH)
    pl.semaphore_wait(barrier, len(peers))


def shift_rows(value, step):
    length = value.shape[1]
    rolled = pltpu.roll(value, step % length, 1)
    at = lax.broadcasted_iota(jnp.int32, value.shape, 1)
    kept = at >= step if step > 0 else at < length + step
    return jnp.where(kept, rolled, 0.0)


def spread_rows(dual):
    return shift_rows(dual, 1) - dual


def row_steps(primal):
    length = primal.shape[1]
    at = lax.broadcasted_iota(jnp.int32, primal.shape, 1)
    return jnp.where(at < length - 1, pltpu.roll(primal, length - 1, 1) - primal, 0.0)


def clipped(value):
    return jnp.minimum(jnp.maximum(value, -1.0), 1.0)


def denoise_frames(target):
    frames = len(target)
    dual_time = [None] * frames
    dual_rows = [None] * frames

    def lowered(frame):
        moved = spread_rows(dual_rows[frame])
        if frame > 0:
            moved = moved + dual_time[frame - 1]
        if frame < frames - 1:
            moved = moved - dual_time[frame]
        return target[frame] - tv_weight * moved

    primal = target
    for repeat in range(INNER):
        if repeat:
            primal = [lowered(frame) for frame in range(frames)]
        for frame in range(frames):
            rows = dual_step * row_steps(primal[frame])
            dual_rows[frame] = clipped(rows if not repeat else dual_rows[frame] + rows)
            if frame < frames - 1:
                time = dual_step * (primal[frame + 1] - primal[frame])
                dual_time[frame] = clipped(time if not repeat else dual_time[frame] + time)
    return [lowered(frame) for frame in range(frames)]


def whole_kernel(
    devices,
    image_ref,
    sens_ref,
    kspace_ref,
    mask_ref,
    rows_ref,
    cols_ref,
    out_ref,
    sens_v,
    image_v,
    rows_v,
    cols_v,
    data_ref,
    mask_v,
    base_ref,
    maps_ref,
    packed_ref,
    landed_ref,
    own_ref,
    now_ref,
    grad_ref,
    gram_ref,
    ready_ref,
    back_ref,
    *rest,
):
    bits = devices.bit_length() - 1
    sums = rest[: bits + 1]
    gots = rest[bits + 1 : 2 * bits + 1]
    (
        load_sem,
        data_sem,
        maps_send,
        maps_recv,
        pack_send,
        pack_recv,
        sum_send,
        sum_recv,
        back_send,
        back_recv,
    ) = rest[2 * bits + 1 :]
    coils, frames, length, packed = base_ref.shape
    rows, all_coils, unused = sens_ref.shape
    half = packed // 2
    low = length // 2
    width = half // devices
    group = LANES // width
    me = lax.axis_index("coil")
    peers = [(me + hop) % devices for hop in range(1, devices)]
    own_bits = [me // (1 << bit) % 2 for bit in range(bits)]
    own_rows = pl.ds(pl.multiple_of(me * rows, SUBLANES), rows)

    loads = []

    def load(source, target):
        loads.append(pltpu.make_async_copy(source, target, load_sem.at[len(loads)]))
        loads[-1].start()

    for coil in range(all_coils):
        load(sens_ref.at[:, coil, :], sens_v.at[coil])
    for frame in range(frames):
        load(image_ref.at[:, frame, :], image_v.at[frame])
    load(rows_ref, rows_v)
    load(cols_ref, cols_v)

    def data_copy(pair, odd):
        return pltpu.make_async_copy(
            kspace_ref.at[:, odd, pair, :], data_ref.at[pair, odd], data_sem.at[pair, odd]
        )

    for pair in range(coils * frames):
        for odd in range(2):
            data_copy(pair, odd).start()

    def remote(source, target, send, recv, peer):
        return pltpu.make_async_remote_copy(
            src_ref=source,
            dst_ref=target,
            send_sem=send,
            recv_sem=recv,
            device_id={"coil": peer},
            device_id_type=MESH,
        )

    def maps_copy(hop, coil):
        peer = peers[hop - 1]
        return remote(
            sens_ref.at[:, peer * coils + coil, :],
            maps_ref.at[coil, own_rows, :],
            maps_send.at[hop - 1, coil],
            maps_recv.at[hop - 1, coil],
            peer,
        )

    def pack_copy(hop):
        peer = peers[hop - 1]
        return remote(
            packed_ref.at[peer],
            landed_ref.at[me],
            pack_send.at[hop - 1],
            pack_recv.at[hop - 1],
            peer,
        )

    def kept_part(stage, frame, other):
        at = own_bits[stage]
        at = 1 - at if other else at
        lead = (slice(None),) * (bits - 1 - stage)
        return sums[stage].at[(frame,) + lead + (at,)]

    def sum_copy(stage, frame):
        return remote(
            kept_part(stage, frame, True),
            gots[stage].at[frame],
            sum_send.at[frame, stage],
            sum_recv.at[frame, stage],
            me + (1 - 2 * own_bits[stage]) * (1 << stage),
        )

    def collect(stage, frame):
        sum_copy(stage, frame).wait_recv()
        sums[stage + 1][frame] = kept_part(stage, frame, False)[...] + gots[stage][frame]

    greet(peers)
    for hop in range(1, devices):
        for coil in range(coils):
            maps_copy(hop, coil).start()
    for copy in loads:
        copy.wait()
    pack_kernel(devices, width, sens_v, image_v, packed_ref)
    for hop in range(1, devices):
        pack_copy(hop).start()
    for coil in range(coils):
        maps_ref[coil, own_rows, :] = sens_v[me * coils + coil]
    landed_ref[me] = packed_ref[me]

    lane = lax.broadcasted_iota(jnp.int32, (length, 2 * length), 1)
    line = lax.broadcasted_iota(jnp.int32, (length, 2 * length), 0)
    picked = line == 2 * (lane % low) + lane // length
    mask_v[...] = dot(
        mask_ref[...].astype(jnp.float32).astype(jnp.bfloat16),
        jnp.where(picked, 1.0, 0.0).astype(jnp.bfloat16),
    )
    for pair in range(coils * frames):
        for odd in range(2):
            data_copy(pair, odd).wait()

    def transform(frame, unused):
        mixes = []
        for odd in range(2):
            weight = mask_v[pl.ds(frame, 1), odd * length : (odd + 1) * length].astype(jnp.bfloat16)
            top, rest_part = (rows_v[odd, 0] * weight, rows_v[odd, 1] * weight)
            mixes.append(jnp.concatenate([rest_part, top, top], 1))
            right = jnp.concatenate([rows_v[odd, 0], rows_v[odd, 1], rows_v[odd, 0]], 1)
            gram = lax.dot_general(
                mixes[-1], right, (((1,), (1,)), ((), ())), preferred_element_type=jnp.float32
            )
            top, rest_part = split(gram)
            gram_ref[frame, odd, 0] = top
            gram_ref[frame, odd, 1] = rest_part
        for coil in range(coils):
            parts = []
            for odd in range(2):
                lines = data_ref[coil * frames + frame, odd]
                lines = jnp.concatenate([lines[:, :half], lines[:, half:]], 0)
                parts.append(dot(mixes[odd], mix_right(split(lines))))
            near, far = (parts[0] + parts[1], parts[0] - parts[1])
            mid = jnp.concatenate(
                [
                    jnp.concatenate([near[:low], near[low:]], 1),
                    jnp.concatenate([far[:low], far[low:]], 1),
                ],
                0,
            )
            base_ref[coil, frame] = dot(mix_left(mid), mix_right(cols_v))
        return unused

    lax.fori_loop(0, frames, transform, 0)
    for hop in range(1, devices):
        for coil in range(coils):
            maps_copy(hop, coil).wait_recv()

    def weigh(frame):
        real, imag = (0.0, 0.0)
        for coil in range(coils):
            base_re, base_im = (base_ref[coil, frame, :, :half], base_ref[coil, frame, :, half:])
            maps_re, maps_im = (maps_ref[coil, :, :half], maps_ref[coil, :, half:])
            real = real + maps_re * base_re + maps_im * base_im
            imag = imag + maps_re * base_im - maps_im * base_re
        shape = (2,) * bits + (width, length)
        lead = (frame,) + (slice(None),) * bits
        sums[0][lead + (slice(0, width),)] = jnp.transpose(real).reshape(shape)
        sums[0][lead + (slice(width, 2 * width),)] = jnp.transpose(imag).reshape(shape)

    def project(frame):
        shape = (all_coils, width, length)
        maps_re, maps_im = (own_ref[0], own_ref[1])
        now_re, now_im = (now_ref[0, frame][None], now_ref[1, frame][None])
        seen_re = (maps_re * now_re - maps_im * now_im).reshape(all_coils * width, length)
        seen_im = (maps_re * now_im + maps_im * now_re).reshape(all_coils * width, length)
        parts = []
        for odd in range(2):
            if odd:
                both = [part[:, :low] - part[:, low:] for part in (seen_re, seen_im)]
            else:
                both = [part[:, :low] + part[:, low:] for part in (seen_re, seen_im)]
            parts.append(dot(mix_left(jnp.concatenate(both, 1)), mix_right(gram_ref[frame, odd])))
        near, far = (parts[0] + parts[1], parts[0] - parts[1])
        kept_re = jnp.concatenate([near[:, :low], far[:, :low]], 1).reshape(shape)
        kept_im = jnp.concatenate([near[:, low:], far[:, low:]], 1).reshape(shape)
        grad_ref[0, frame] = jnp.sum(maps_re * kept_re + maps_im * kept_im, 0)
        grad_ref[1, frame] = jnp.sum(maps_re * kept_im - maps_im * kept_re, 0)

    for turn in range(frames + 2):
        if turn < frames:
            weigh(turn)
            sum_copy(0, turn).start()
        for stage in range(2):
            frame = turn - 1 - stage
            if 0 <= frame < frames:
                collect(stage, frame)
                sum_copy(stage + 1, frame).start()

    for hop in range(1, devices):
        pack_copy(hop).wait_recv()
    cut = 2 * all_coils * width
    turned = jnp.transpose(landed_ref[...].reshape(length, landed_ref.shape[2]))
    own_ref[...] = turned[:cut].reshape(own_ref.shape)
    now_ref[...] = turned[cut:].reshape(now_ref.shape)
    for frame in range(frames):
        project(frame)
        collect(2, frame)
        for stage in range(3, bits):
            sum_copy(stage, frame).start()
            if stage < bits - 1:
                collect(stage, frame)
    for frame in range(frames):
        collect(bits - 1, frame)

    for sweep in range(OUTER):
        if sweep:
            for frame in range(frames):
                project(frame)
        for part in range(2):
            target = []
            for frame in range(frames):
                data_term = sums[bits][frame, part * width : (part + 1) * width]
                gradient = grad_ref[part, frame] - data_term
                target.append(now_ref[part, frame] - step_size * gradient)
            for frame, value in enumerate(denoise_frames(target)):
                now_ref[part, frame] = value

    turned = jnp.transpose(now_ref[...].reshape(2 * frames * width, length))
    ready_ref[...] = turned.reshape(ready_ref.shape)

    def back_copy(hop):
        peer = peers[hop - 1]
        return remote(
            ready_ref.at[peer], back_ref.at[me], back_send.at[hop - 1], back_recv.at[hop - 1], peer
        )

    for hop in range(1, devices):
        back_copy(hop).start()
    back_ref[me] = ready_ref[me]
    for hop in range(1, devices):
        back_copy(hop).wait_recv()
    for part in range(2):
        for first in range(0, frames, group):
            lane = (part * frames + first) * width
            for tile in range(devices // group):
                taken = [
                    back_ref[tile * group + at, :, lane : lane + LANES] for at in range(group)
                ]
                target = part * half + tile * LANES
                for at, value in enumerate(swap_blocks(taken, width)):
                    out_ref[:, first + at, target : target + LANES] = value
    for hop in range(1, devices):
        for coil in range(coils):
            maps_copy(hop, coil).wait_send()
        pack_copy(hop).wait_send()
        back_copy(hop).wait_send()
    for frame in range(frames):
        for stage in range(bits):
            sum_copy(stage, frame).wait_send()


def reconstruct(image, sens, kspace, mask, devices):
    rows, frames, packed = image.shape
    all_coils = sens.shape[1]
    length, pairs, unused = kspace.shape
    coils = pairs // frames
    bits = devices.bit_length() - 1
    width = packed // 2 // devices
    lanes = 2 * (all_coils + frames) * width
    row_pairs = row_tables(length)
    col_pair = column_table(packed // 2)
    whole = pl.BlockSpec(memory_space=pltpu.VMEM)
    apart = pl.BlockSpec(memory_space=pl.ANY)

    def held(*shape):
        return pltpu.VMEM(shape, jnp.float32)

    dma = pltpu.SemaphoreType.DMA
    block = (2 * width, length)
    sums = [held(frames, *(2,) * (bits - stage), *block) for stage in range(bits + 1)]
    gots = [held(frames, *(2,) * (bits - 1 - stage), *block) for stage in range(bits)]
    return pl.pallas_call(
        lambda *refs: whole_kernel(devices, *refs),
        out_shape=jax.ShapeDtypeStruct((rows, frames, packed), jnp.float32),
        in_specs=[apart] * 3 + [whole] + [apart] * 2,
        out_specs=whole,
        scratch_shapes=[
            held(all_coils, rows, packed),
            held(frames, rows, packed),
            pltpu.VMEM(row_pairs.shape, jnp.bfloat16),
            pltpu.VMEM(col_pair.shape, jnp.bfloat16),
            held(pairs, 2, length // 2, packed),
            held(frames, 2 * length),
            held(coils, frames, length, packed),
            held(coils, length, packed),
            held(devices, rows, lanes),
            held(devices, rows, lanes),
            held(2, all_coils, width, length),
            held(2, frames, width, length),
            held(2, frames, width, length),
            pltpu.VMEM((frames, 2, 2, length, length), jnp.bfloat16),
            held(devices, rows, 2 * frames * width),
            held(devices, rows, 2 * frames * width),
            *sums,
            *gots,
            dma((all_coils + frames + 2,)),
            dma((pairs, 2)),
            dma((devices - 1, coils)),
            dma((devices - 1, coils)),
            dma((devices - 1,)),
            dma((devices - 1,)),
            dma((frames, bits)),
            dma((frames, bits)),
            dma((devices - 1,)),
            dma((devices - 1,)),
        ],
        compiler_params=pltpu.CompilerParams(
            collective_id=0, has_side_effects=True, vmem_limit_bytes=60 * 1024 * 1024
        ),
        name="reconstruct",
    )(
        image,
        sens,
        kspace.reshape(length // 2, 2, pairs, packed),
        mask,
        jnp.asarray(row_pairs),
        jnp.asarray(col_pair),
    )


def per_device(image, sens, kspace, mask):
    devices = lax.axis_size("coil")
    device = lax.axis_index("coil")
    rows_dev, frames, packed = image.shape
    coils = sens.shape[1]
    length, pairs, unused = kspace.shape
    half = packed // 2
    width = half // devices
    copies = max(1, frames // pairs)
    own_coils = max(1, pairs // frames)
    own_frames = min(frames, pairs)
    if blocked(devices, width, rows_dev, length, half, coils, frames, pairs):
        return reconstruct(image, sens, kspace, mask, devices)
    row_cos, row_sin = dft_tables(length)
    col_cos, col_sin = dft_tables(half)
    mask_float = mask.astype(jnp.float32)
    real, imag = projections(mask, row_cos, row_sin)
    spread = sens if copies == 1 else jnp.repeat(sens, copies, axis=1)
    own_maps = lax.all_to_all(spread, "coil", split_axis=1, concat_axis=0, tiled=True)
    outgoing = jnp.concatenate([to_columns(sens, devices), to_columns(image, devices)], 2)
    incoming = lax.all_to_all(outgoing, "coil", split_axis=0, concat_axis=0, tiled=True)
    columns = jnp.transpose(incoming.reshape(length, -1))
    first_frame = device * pairs % frames
    local_mask = lax.dynamic_slice_in_dim(mask_float, first_frame, own_frames, 0)
    mask_pairs = jnp.tile(local_mask, (own_coils, 1))
    base_re, base_im = data_images(kspace, mask_pairs, row_cos, row_sin, col_cos, col_sin)
    base_re = base_re.reshape(length, own_coils, own_frames, half)
    base_im = base_im.reshape(length, own_coils, own_frames, half)
    own_re, own_im = (own_maps[:, :, None, :half], own_maps[:, :, None, half:])
    term_re = jnp.sum(own_re * base_re + own_im * base_im, 1)
    term_im = jnp.sum(own_re * base_im - own_im * base_re, 1)
    term = jnp.transpose(jnp.stack([term_re, term_im]), (3, 0, 2, 1))
    if own_frames < frames:
        wide = jnp.zeros((half, 2, frames, length), jnp.float32)
        term = lax.dynamic_update_slice_in_dim(wide, term, first_frame, 2)
    term = term.reshape(devices, width, 2, frames, length)
    data_term = lax.psum_scatter(term, "coil", scatter_dimension=0, tiled=True)
    data_term = jnp.transpose(data_term[0], (1, 2, 0, 3))

    cut = 2 * coils * width
    maps = columns[:cut].reshape(2, coils, width, length)
    field = columns[cut:].reshape(2, frames, width, length)
    field = iterate(field, data_term, maps, real, imag)

    leaving = jnp.transpose(field.reshape(2 * frames * width, length))
    leaving = leaving.reshape(devices, rows_dev, 2 * frames * width)
    arrived = lax.all_to_all(leaving, "coil", split_axis=0, concat_axis=0, tiled=True)
    arrived = arrived.reshape(devices, rows_dev, 2, frames, width)
    return jnp.transpose(arrived, (1, 3, 2, 0, 4)).reshape(rows_dev, frames, packed)


def solution(mesh):
    return jax.shard_map(
        per_device,
        mesh=mesh,
        in_specs=(
            P(("plane", "coil"), None, None),
            P(("plane", "coil"), None, None),
            P("plane", "coil", None),
            P(),
        ),
        out_specs=P(("plane", "coil"), None, None),
        check_vma=False,
    )
```

profile of v0, /device:TPU:0, one launch (start us, length us, event | category | flops | bytes accessed | tf_op | source)
XLA Modules:
  0.0 98.9 jit_solution(3275168712414545572)
XLA Ops:
  0.0 97.2 %reconstruct.1 = f32[16,8,512]{2,1,0:T(8,128)} custom-call(f32[16,8,512]{2,1,0:T(8,128)} %refs_0_.1, f32[16,32,512]{2,1,0:T(8,128)} %refs_1_.1, f32[128,2,16,512]{3,2,1,0:T(8,128)} %bitcast.1, s32[8,256]{1,0:T(8,128)} %refs_3_.1, bf16[2,2,256,256]{3,2,1,0:T(8,128)(2,1)} %constant.4.clone.refs_4_, bf16[2,512,512]{2,1,0:T(8,128)(2,1)} %constant.5.clone.refs_5_), custom_call_target="tpu_custom_call" | custom-call | tf_op jit(solution)/shard_map/reconstruct/pallas_call | solution.py:577
  97.2 1.7 %copy.8 = f32[16,8,512]{2,1,0:T(8,128)} copy(f32[16,8,512]{2,1,0:T(8,128)} %reconstruct.1) | data formatting | bytes 524288
where the time goes:
time: 99.8 us; the launch traced here: 98.9 us
  Pallas kernels  97.2 us (97%)
  local copies, waits for them, and re-layouts  1.67 us (2%)
    pallas_call x1, Pallas kernels, reconstruct(): pl.pallas_call(lambda *refs: whole_kernel(devices, *refs), out_shape=jax....  97.2 us

commit v1 on v0

--- a/solution.py
+++ b/solution.py
@@ -145,23 +145,29 @@
 def blocked(devices, width, rows, length, half, coils, frames, pairs):
     group = LANES // width
     fits = LANES % width == 0 and width % SUBLANES == 0 and rows % SUBLANES == 0
-    fits = fits and devices % group == 0 and coils % group == 0 and frames % group == 0
-    fits = fits and devices >= SUBLANES and devices & (devices - 1) == 0
-    fits = fits and pairs % frames == 0 and coils * frames == pairs * devices
-    return fits and length % (2 * LANES) == 0 and half % LANES == 0
+    fits = fits and devices % group == 0 and coils % (2 * group) == 0 and frames % group == 0
+    fits = fits and devices & (devices - 1) == 0
+    fits = fits and devices >= 16 and pairs % frames == 0 and coils * frames == pairs * devices
+    return fits and length % (2 * LANES) == 0 and half % (2 * LANES) == 0
 
 
 def pack_kernel(devices, width, sens_ref, image_ref, out_ref):
     group = LANES // width
     half = devices * width
+    near = sens_ref.shape[0] // 2
     start = 0
-    for source in (sens_ref, image_ref):
-        count = source.shape[0]
+    for source, origin, count in (
+        (sens_ref, 0, near),
+        (image_ref, 0, image_ref.shape[0]),
+        (sens_ref, near, near),
+    ):
         for part in range(2):
             for tile in range(half // LANES):
                 lane = part * half + tile * LANES
                 for first in range(0, count, group):
-                    taken = [source[first + at, :, lane : lane + LANES] for at in range(group)]
+                    taken = [
+                        source[origin + first + at, :, lane : lane + LANES] for at in range(group)
+                    ]
                     target = start + (part * count + first) * width
                     for at, value in enumerate(swap_blocks(taken, width)):
                         out_ref[tile * group + at, :, target : target + LANES] = value
@@ -290,6 +296,7 @@
     now_ref,
     grad_ref,
     gram_ref,
+    relay_ref,
     ready_ref,
     back_ref,
     *rest,
@@ -304,6 +311,8 @@
         maps_recv,
         pack_send,
         pack_recv,
+        relay_send,
+        relay_recv,
         sum_send,
         sum_recv,
         back_send,
@@ -316,8 +325,18 @@
     width = half // devices
     group = LANES // width
     me = lax.axis_index("coil")
-    peers = [(me + hop) % devices for hop in range(1, devices)]
     own_bits = [me // (1 << bit) % 2 for bit in range(bits)]
+    peers = []
+    for hop in range(1, devices):
+        flips = [(own_bits[bit] + (hop >> bit)) % 2 * (1 << bit) for bit in range(bits)]
+        peers.append(sum(flips[1:], flips[0]))
+    near = devices // 2
+    side = me // near
+    far_side = 1 - side
+    near_hops = list(range(1, near))
+    far_hops = list(range(near, devices))
+    block = all_coils * width
+    held_lanes = 2 * frames * width
     own_rows = pl.ds(pl.multiple_of(me * rows, SUBLANES), rows)
 
     loads = []
@@ -364,11 +383,29 @@
 
     def pack_copy(hop):
         peer = peers[hop - 1]
+        if hop < near:
+            lanes = pl.ds(0, 2 * block + held_lanes)
+        else:
+            lanes = pl.ds(pl.multiple_of(side * block, LANES), block + held_lanes)
         return remote(
-            packed_ref.at[peer],
-            landed_ref.at[me],
+            packed_ref.at[peer, :, lanes],
+            landed_ref.at[me, :, lanes],
             pack_send.at[hop - 1],
             pack_recv.at[hop - 1],
+            peer,
+        )
+
+    def relay_part(coil_side, first, row_side):
+        lanes = pl.ds(pl.multiple_of(row_side * low, LANES), low)
+        return own_ref.at[coil_side, :, pl.ds(first, coils), :, lanes]
+
+    def relay_copy(hop):
+        peer = peers[hop - 1]
+        return remote(
+            relay_ref.at[peer % near],
+            relay_part(side, me % near * coils, far_side),
+            relay_send.at[hop - 1],
+            relay_recv.at[hop - 1],
             peer,
         )
 
@@ -392,13 +429,24 @@
         sums[stage + 1][frame] = kept_part(stage, frame, False)[...] + gots[stage][frame]
 
     greet(peers)
-    for hop in range(1, devices):
-        for coil in range(coils):
-            maps_copy(hop, coil).start()
+    early = near // 2
+    for far_hop, near_hop in zip(far_hops[:early], near_hops[:early]):
+        for hop in (far_hop, near_hop):
+            for coil in range(coils):
+                maps_copy(hop, coil).start()
     for copy in loads:
         copy.wait()
     pack_kernel(devices, width, sens_v, image_v, packed_ref)
-    for hop in range(1, devices):
+    for at in range(near):
+        if at < early:
+            for coil in range(coils):
+                maps_copy(far_hops[early + at], coil).start()
+        if early <= at < near - 1:
+            for coil in range(coils):
+                maps_copy(near_hops[at], coil).start()
+        if at < near - 1:
+            pack_copy(near_hops[at]).start()
+    for hop in far_hops:
         pack_copy(hop).start()
     for coil in range(coils):
         maps_ref[coil, own_rows, :] = sens_v[me * coils + coil]
@@ -464,7 +512,7 @@
 
     def project(frame):
         shape = (all_coils, width, length)
-        maps_re, maps_im = (own_ref[0], own_ref[1])
+        maps_re, maps_im = (own_ref[:, 0].reshape(shape), own_ref[:, 1].reshape(shape))
         now_re, now_im = (now_ref[0, frame][None], now_ref[1, frame][None])
         seen_re = (maps_re * now_re - maps_im * now_im).reshape(all_coils * width, length)
         seen_im = (maps_re * now_im + maps_im * now_re).reshape(all_coils * width, length)
@@ -481,30 +529,48 @@
         grad_ref[0, frame] = jnp.sum(maps_re * kept_re + maps_im * kept_im, 0)
         grad_ref[1, frame] = jnp.sum(maps_re * kept_im - maps_im * kept_re, 0)
 
-    for turn in range(frames + 2):
+    def turn_maps():
+        lines = pl.ds(pl.multiple_of(far_side * low, LANES), low)
+        for coil in range(coils):
+            for part in range(2):
+                lanes = pl.ds(pl.multiple_of(part * half + side * (half // 2), LANES), half // 2)
+                turned = jnp.transpose(maps_ref[coil, lines, lanes])
+                relay_ref[:, part, coil] = turned.reshape(near, width, low)
+        for hop in near_hops:
+            relay_copy(hop).start()
+        relay_part(side, me % near * coils, far_side)[...] = relay_ref[me % near]
+
+    lags = [1, 2] + [2 + 2 * stage for stage in range(1, bits - 2)]
+    for turn in range(frames + lags[-1]):
         if turn < frames:
             weigh(turn)
             sum_copy(0, turn).start()
-        for stage in range(2):
-            frame = turn - 1 - stage
-            if 0 <= frame < frames:
-                collect(stage, frame)
-                sum_copy(stage + 1, frame).start()
+        for stage, lag in enumerate(lags):
+            if 0 <= turn - lag < frames:
+                collect(stage, turn - lag)
+                sum_copy(stage + 1, turn - lag).start()
+        if turn == 0:
+            turn_maps()
 
     for hop in range(1, devices):
         pack_copy(hop).wait_recv()
-    cut = 2 * all_coils * width
-    turned = jnp.transpose(landed_ref[...].reshape(length, landed_ref.shape[2]))
-    own_ref[...] = turned[:cut].reshape(own_ref.shape)
-    now_ref[...] = turned[cut:].reshape(now_ref.shape)
+    for hop in near_hops:
+        relay_copy(hop).wait_recv()
+
+    def unfold(target, row_side, lines, lanes):
+        turned = jnp.transpose(landed_ref[lines, :, lanes].reshape(low, -1))
+        rows_at = pl.ds(pl.multiple_of(row_side * low, LANES), low)
+        target[..., rows_at] = turned.reshape(target.shape[:-1] + (low,))
+
+    for row_side in (side, far_side):
+        lines = pl.ds(row_side * near, near)
+        unfold(now_ref, row_side, lines, pl.ds(block, held_lanes))
+    for coil_side, row_side in ((0, side), (1, side), (far_side, far_side)):
+        start = pl.multiple_of(coil_side * (block + held_lanes), LANES)
+        lines = pl.ds(row_side * near, near)
+        unfold(own_ref.at[coil_side], row_side, lines, pl.ds(start, block))
     for frame in range(frames):
         project(frame)
-        collect(2, frame)
-        for stage in range(3, bits):
-            sum_copy(stage, frame).start()
-            if stage < bits - 1:
-                collect(stage, frame)
-    for frame in range(frames):
         collect(bits - 1, frame)
 
     for sweep in range(OUTER):
@@ -548,6 +614,8 @@
         for coil in range(coils):
             maps_copy(hop, coil).wait_send()
         pack_copy(hop).wait_send()
+        if hop < near:
+            relay_copy(hop).wait_send()
         back_copy(hop).wait_send()
     for frame in range(frames):
         for stage in range(bits):
@@ -590,10 +658,11 @@
             held(coils, length, packed),
             held(devices, rows, lanes),
             held(devices, rows, lanes),
-            held(2, all_coils, width, length),
+            held(2, 2, all_coils // 2, width, length),
             held(2, frames, width, length),
             held(2, frames, width, length),
             pltpu.VMEM((frames, 2, 2, length, length), jnp.bfloat16),
+            held(devices // 2, 2, coils, width, length // 2),
             held(devices, rows, 2 * frames * width),
             held(devices, rows, 2 * frames * width),
             *sums,
@@ -604,6 +673,8 @@
             dma((devices - 1, coils)),
             dma((devices - 1,)),
             dma((devices - 1,)),
+            dma((devices // 2 - 1,)),
+            dma((devices // 2 - 1,)),
             dma((frames, bits)),
             dma((frames, bits)),
             dma((devices - 1,)),

time: 99.8 us -> 93.1 us (0.933)
  Pallas kernels: 97.2 us -> 91.3 us
    pallas_call x1, Pallas kernels: 97.2 us -> 91.3 us  [reconstruct(): pl.pallas_call(lambda *refs: whole_kernel(devices, *refs), out_shape=jax....]
where the time goes in v1:
time: 93.1 us; the launch traced here: 93 us
  Pallas kernels  91.3 us (98%)
  local copies, waits for them, and re-layouts  1.67 us (2%)
    pallas_call x1, Pallas kernels, reconstruct(): pl.pallas_call(lambda *refs: whole_kernel(devices, *refs), out_shape=jax....  91.3 us

profile of v1, /device:TPU:0, one launch (start us, length us, event | category | flops | bytes accessed | tf_op | source)
XLA Modules:
  0.0 93.0 jit_solution(1068576890718755529)
XLA Ops:
  0.0 91.3 %reconstruct.1 = f32[16,8,512]{2,1,0:T(8,128)} custom-call(f32[16,8,512]{2,1,0:T(8,128)} %refs_0_.1, f32[16,32,512]{2,1,0:T(8,128)} %refs_1_.1, f32[128,2,16,512]{3,2,1,0:T(8,128)} %bitcast.1, s32[8,256]{1,0:T(8,128)} %refs_3_.1, bf16[2,2,256,256]{3,2,1,0:T(8,128)(2,1)} %constant.4.clone.refs_4_, bf16[2,512,512]{2,1,0:T(8,128)(2,1)} %constant.5.clone.refs_5_), custom_call_target="tpu_custom_call" | custom-call | tf_op jit(solution)/shard_map/reconstruct/pallas_call | solution.py:645
  91.3 1.7 %copy.8 = f32[16,8,512]{2,1,0:T(8,128)} copy(f32[16,8,512]{2,1,0:T(8,128)} %reconstruct.1) | data formatting | bytes 524288

commit v2 on v1

--- a/solution.py
+++ b/solution.py
@@ -297,13 +297,14 @@
     grad_ref,
     gram_ref,
     relay_ref,
+    total_ref,
     ready_ref,
     back_ref,
     *rest,
 ):
     bits = devices.bit_length() - 1
-    sums = rest[: bits + 1]
-    gots = rest[bits + 1 : 2 * bits + 1]
+    sums = rest[:bits]
+    gots = rest[bits : 2 * bits]
     (
         load_sem,
         data_sem,
@@ -317,7 +318,7 @@
         sum_recv,
         back_send,
         back_recv,
-    ) = rest[2 * bits + 1 :]
+    ) = rest[2 * bits :]
     coils, frames, length, packed = base_ref.shape
     rows, all_coils, unused = sens_ref.shape
     half = packed // 2
@@ -409,45 +410,51 @@
             peer,
         )
 
-    def kept_part(stage, frame, other):
+    def kept_part(stage, phase, frame, other):
         at = own_bits[stage]
         at = 1 - at if other else at
         lead = (slice(None),) * (bits - 1 - stage)
-        return sums[stage].at[(frame,) + lead + (at,)]
-
-    def sum_copy(stage, frame):
+        return sums[stage].at[(phase, frame) + lead + (at,)]
+
+    def sum_copy(stage, phase, frame):
+        landing = 1 - phase if stage == bits - 1 else phase
         return remote(
-            kept_part(stage, frame, True),
-            gots[stage].at[frame],
-            sum_send.at[frame, stage],
-            sum_recv.at[frame, stage],
+            kept_part(stage, phase, frame, True),
+            gots[stage].at[landing, frame],
+            sum_send.at[phase, frame, stage],
+            sum_recv.at[landing, frame, stage],
             me + (1 - 2 * own_bits[stage]) * (1 << stage),
         )
 
-    def collect(stage, frame):
-        sum_copy(stage, frame).wait_recv()
-        sums[stage + 1][frame] = kept_part(stage, frame, False)[...] + gots[stage][frame]
+    def side_rows(phase):
+        row_side = far_side if phase else side
+        return pl.ds(pl.multiple_of(row_side * low, LANES), low)
+
+    def collect(stage, phase, frame):
+        last = stage == bits - 1
+        sum_copy(stage, 1 - phase if last else phase, frame).wait_recv()
+        total = kept_part(stage, phase, frame, False)[...] + gots[stage][phase, frame]
+        if last:
+            total_ref[frame, :, side_rows(phase)] = total
+        else:
+            sums[stage + 1][phase, frame] = total
 
     greet(peers)
     early = near // 2
-    for far_hop, near_hop in zip(far_hops[:early], near_hops[:early]):
-        for hop in (far_hop, near_hop):
-            for coil in range(coils):
-                maps_copy(hop, coil).start()
+    for hop in near_hops + far_hops[:early]:
+        for coil in range(coils):
+            maps_copy(hop, coil).start()
     for copy in loads:
         copy.wait()
     pack_kernel(devices, width, sens_v, image_v, packed_ref)
-    for at in range(near):
+    for at in range(near - 1):
         if at < early:
             for coil in range(coils):
                 maps_copy(far_hops[early + at], coil).start()
-        if early <= at < near - 1:
-            for coil in range(coils):
-                maps_copy(near_hops[at], coil).start()
-        if at < near - 1:
-            pack_copy(near_hops[at]).start()
+        pack_copy(near_hops[at]).start()
     for hop in far_hops:
-        pack_copy(hop).start()
+        if hop // 2 % 2 == 0:
+            pack_copy(hop).start()
     for coil in range(coils):
         maps_ref[coil, own_rows, :] = sens_v[me * coils + coil]
     landed_ref[me] = packed_ref[me]
@@ -463,7 +470,7 @@
         for odd in range(2):
             data_copy(pair, odd).wait()
 
-    def transform(frame, unused):
+    def transform(frame):
         mixes = []
         for odd in range(2):
             weight = mask_v[pl.ds(frame, 1), odd * length : (odd + 1) * length].astype(jnp.bfloat16)
@@ -491,24 +498,66 @@
                 0,
             )
             base_ref[coil, frame] = dot(mix_left(mid), mix_right(cols_v))
+
+    def weigh(phase, frame):
+        real, imag = (0.0, 0.0)
+        lines = side_rows(phase)
+        for coil in range(coils):
+            base_re, base_im = (
+                base_ref[coil, frame, lines, :half],
+                base_ref[coil, frame, lines, half:],
+            )
+            maps_re, maps_im = (maps_ref[coil, lines, :half], maps_ref[coil, lines, half:])
+            real = real + maps_re * base_re + maps_im * base_im
+            imag = imag + maps_re * base_im - maps_im * base_re
+        shape = (2,) * bits + (width, low)
+        lead = (phase, frame) + (slice(None),) * bits
+        sums[0][lead + (slice(0, width),)] = jnp.transpose(real).reshape(shape)
+        sums[0][lead + (slice(width, 2 * width),)] = jnp.transpose(imag).reshape(shape)
+
+    def pass_on(stage, phase, frame):
+        if 0 <= frame < frames:
+            collect(stage, phase, frame)
+            sum_copy(stage + 1, phase, frame).start()
+
+    def offer(phase, frame):
+        if frame < frames:
+            weigh(phase, frame)
+            sum_copy(0, phase, frame).start()
+        pass_on(0, phase, frame - 1)
+
+    lead = min(3, frames - 1)
+
+    def step(frame, unused):
+        transform(frame)
+
+        @pl.when(frame == lead)
+        def wait_near():
+            for hop in near_hops:
+                for coil in range(coils):
+                    maps_copy(hop, coil).wait_recv()
+
+        @pl.when(frame >= lead)
+        def offer_near():
+            weigh(0, frame - lead)
+            sum_copy(0, 0, frame - lead).start()
+
+        @pl.when(frame > lead)
+        def pass_near():
+            collect(0, 0, frame - lead - 1)
+            sum_copy(1, 0, frame - lead - 1).start()
+
         return unused
 
-    lax.fori_loop(0, frames, transform, 0)
-    for hop in range(1, devices):
+    lax.fori_loop(0, frames, step, 0)
+    for turn in range(frames - lead, frames + 1):
+        offer(0, turn)
+    for hop in far_hops:
+        if hop // 2 % 2:
+            pack_copy(hop).start()
+    for hop in far_hops:
         for coil in range(coils):
             maps_copy(hop, coil).wait_recv()
-
-    def weigh(frame):
-        real, imag = (0.0, 0.0)
-        for coil in range(coils):
-            base_re, base_im = (base_ref[coil, frame, :, :half], base_ref[coil, frame, :, half:])
-            maps_re, maps_im = (maps_ref[coil, :, :half], maps_ref[coil, :, half:])
-            real = real + maps_re * base_re + maps_im * base_im
-            imag = imag + maps_re * base_im - maps_im * base_re
-        shape = (2,) * bits + (width, length)
-        lead = (frame,) + (slice(None),) * bits
-        sums[0][lead + (slice(0, width),)] = jnp.transpose(real).reshape(shape)
-        sums[0][lead + (slice(width, 2 * width),)] = jnp.transpose(imag).reshape(shape)
 
     def project(frame):
         shape = (all_coils, width, length)
@@ -540,38 +589,48 @@
             relay_copy(hop).start()
         relay_part(side, me % near * coils, far_side)[...] = relay_ref[me % near]
 
-    lags = [1, 2] + [2 + 2 * stage for stage in range(1, bits - 2)]
-    for turn in range(frames + lags[-1]):
-        if turn < frames:
-            weigh(turn)
-            sum_copy(0, turn).start()
-        for stage, lag in enumerate(lags):
-            if 0 <= turn - lag < frames:
-                collect(stage, turn - lag)
-                sum_copy(stage + 1, turn - lag).start()
-        if turn == 0:
-            turn_maps()
-
-    for hop in range(1, devices):
-        pack_copy(hop).wait_recv()
-    for hop in near_hops:
-        relay_copy(hop).wait_recv()
-
     def unfold(target, row_side, lines, lanes):
         turned = jnp.transpose(landed_ref[lines, :, lanes].reshape(low, -1))
         rows_at = pl.ds(pl.multiple_of(row_side * low, LANES), low)
         target[..., rows_at] = turned.reshape(target.shape[:-1] + (low,))
 
-    for row_side in (side, far_side):
-        lines = pl.ds(row_side * near, near)
-        unfold(now_ref, row_side, lines, pl.ds(block, held_lanes))
-    for coil_side, row_side in ((0, side), (1, side), (far_side, far_side)):
-        start = pl.multiple_of(coil_side * (block + held_lanes), LANES)
-        lines = pl.ds(row_side * near, near)
-        unfold(own_ref.at[coil_side], row_side, lines, pl.ds(start, block))
-    for frame in range(frames):
+    def take_columns():
+        for hop in range(1, devices):
+            pack_copy(hop).wait_recv()
+        for hop in near_hops:
+            relay_copy(hop).wait_recv()
+        for row_side in (side, far_side):
+            lines = pl.ds(row_side * near, near)
+            unfold(now_ref, row_side, lines, pl.ds(block, held_lanes))
+        for coil_side, row_side in ((0, side), (1, side), (far_side, far_side)):
+            start = pl.multiple_of(coil_side * (block + held_lanes), LANES)
+            lines = pl.ds(row_side * near, near)
+            unfold(own_ref.at[coil_side], row_side, lines, pl.ds(start, block))
+
+    for turn in range(frames + 1):
+        offer(1, turn)
+        if turn == 0:
+            turn_maps()
+        pass_on(1, 0, turn)
+    for stage in range(2, bits - 2):
+        for turn in range(frames):
+            pass_on(stage - 1, 1, turn)
+            pass_on(stage, 0, turn)
+    first = min(1, frames - 1)
+    for turn in range(frames + 2):
+        if turn < frames:
+            pass_on(bits - 3, 1, turn)
+            pass_on(bits - 2, 0, turn)
+        pass_on(bits - 2, 1, turn - 2)
+        if turn == first:
+            take_columns()
+        if first <= turn < frames:
+            project(turn - first)
+    for frame in range(frames - first, frames):
         project(frame)
-        collect(bits - 1, frame)
+    for phase in range(2):
+        for frame in range(frames):
+            collect(bits - 1, phase, frame)
 
     for sweep in range(OUTER):
         if sweep:
@@ -580,7 +639,7 @@
         for part in range(2):
             target = []
             for frame in range(frames):
-                data_term = sums[bits][frame, part * width : (part + 1) * width]
+                data_term = total_ref[frame, part * width : (part + 1) * width]
                 gradient = grad_ref[part, frame] - data_term
                 target.append(now_ref[part, frame] - step_size * gradient)
             for frame, value in enumerate(denoise_frames(target)):
@@ -619,7 +678,8 @@
         back_copy(hop).wait_send()
     for frame in range(frames):
         for stage in range(bits):
-            sum_copy(stage, frame).wait_send()
+            for phase in range(2):
+                sum_copy(stage, phase, frame).wait_send()
 
 
 def reconstruct(image, sens, kspace, mask, devices):
@@ -639,9 +699,9 @@
         return pltpu.VMEM(shape, jnp.float32)
 
     dma = pltpu.SemaphoreType.DMA
-    block = (2 * width, length)
-    sums = [held(frames, *(2,) * (bits - stage), *block) for stage in range(bits + 1)]
-    gots = [held(frames, *(2,) * (bits - 1 - stage), *block) for stage in range(bits)]
+    block = (2 * width, length // 2)
+    sums = [held(2, frames, *(2,) * (bits - stage), *block) for stage in range(bits)]
+    gots = [held(2, frames, *(2,) * (bits - 1 - stage), *block) for stage in range(bits)]
     return pl.pallas_call(
         lambda *refs: whole_kernel(devices, *refs),
         out_shape=jax.ShapeDtypeStruct((rows, frames, packed), jnp.float32),
@@ -663,6 +723,7 @@
             held(2, frames, width, length),
             pltpu.VMEM((frames, 2, 2, length, length), jnp.bfloat16),
             held(devices // 2, 2, coils, width, length // 2),
+            held(frames, 2 * width, length),
             held(devices, rows, 2 * frames * width),
             held(devices, rows, 2 * frames * width),
             *sums,
@@ -675,8 +736,8 @@
             dma((devices - 1,)),
             dma((devices // 2 - 1,)),
             dma((devices // 2 - 1,)),
-            dma((frames, bits)),
-            dma((frames, bits)),
+            dma((2, frames, bits)),
+            dma((2, frames, bits)),
             dma((devices - 1,)),
             dma((devices - 1,)),
         ],

time: 93.1 us -> 84.3 us (0.905)
  Pallas kernels: 91.3 us -> 82.4 us
    pallas_call x1, Pallas kernels: 91.3 us -> 82.4 us  [reconstruct(): pl.pallas_call(lambda *refs: whole_kernel(devices, *refs), out_shape=jax....]
where the time goes in v2:
time: 84.3 us; the launch traced here: 84.1 us
  Pallas kernels  82.4 us (98%)
  local copies, waits for them, and re-layouts  1.67 us (2%)
    pallas_call x1, Pallas kernels, reconstruct(): pl.pallas_call(lambda *refs: whole_kernel(devices, *refs), out_shape=jax....  82.4 us

profile of v2, /device:TPU:0, one launch (start us, length us, event | category | flops | bytes accessed | tf_op | source)
XLA Modules:
  0.0 84.1 jit_solution(5011918284447709773)
XLA Ops:
  0.0 82.4 %reconstruct.1 = f32[16,8,512]{2,1,0:T(8,128)} custom-call(f32[16,8,512]{2,1,0:T(8,128)} %refs_0_.1, f32[16,32,512]{2,1,0:T(8,128)} %refs_1_.1, f32[128,2,16,512]{3,2,1,0:T(8,128)} %bitcast.1, s32[8,256]{1,0:T(8,128)} %refs_3_.1, bf16[2,2,256,256]{3,2,1,0:T(8,128)(2,1)} %constant.4.clone.refs_4_, bf16[2,512,512]{2,1,0:T(8,128)(2,1)} %constant.5.clone.refs_5_), custom_call_target="tpu_custom_call" | custom-call | tf_op jit(solution)/shard_map/reconstruct/pallas_call | solution.py:705
  82.4 1.7 %copy.8 = f32[16,8,512]{2,1,0:T(8,128)} copy(f32[16,8,512]{2,1,0:T(8,128)} %reconstruct.1) | data formatting | bytes 524288

commit v3 on v2

--- a/solution.py
+++ b/solution.py
@@ -147,7 +147,7 @@
     fits = LANES % width == 0 and width % SUBLANES == 0 and rows % SUBLANES == 0
     fits = fits and devices % group == 0 and coils % (2 * group) == 0 and frames % group == 0
     fits = fits and devices & (devices - 1) == 0
-    fits = fits and devices >= 16 and pairs % frames == 0 and coils * frames == pairs * devices
+    fits = fits and devices >= 16 and frames % 2 == 0 and pairs % frames == 0 and coils * frames == pairs * devices
     return fits and length % (2 * LANES) == 0 and half % (2 * LANES) == 0
 
 
@@ -218,11 +218,15 @@
 MESH = pl.DeviceIdType.MESH
 
 
-def greet(peers):
-    barrier = pltpu.get_barrier_semaphore()
+def announce(peers):
     for peer in peers:
-        pl.semaphore_signal(barrier, 1, device_id={"coil": peer}, device_id_type=MESH)
-    pl.semaphore_wait(barrier, len(peers))
+        pl.semaphore_signal(
+            pltpu.get_barrier_semaphore(), 1, device_id={"coil": peer}, device_id_type=MESH
+        )
+
+
+def drain(whole, sem):
+    pltpu.make_async_copy(whole, whole, sem).wait()
 
 
 def shift_rows(value, step):
@@ -307,7 +311,6 @@
     gots = rest[bits : 2 * bits]
     (
         load_sem,
-        data_sem,
         maps_send,
         maps_recv,
         pack_send,
@@ -332,6 +335,7 @@
         flips = [(own_bits[bit] + (hop >> bit)) % 2 * (1 << bit) for bit in range(bits)]
         peers.append(sum(flips[1:], flips[0]))
     near = devices // 2
+    some = frames // 2
     side = me // near
     far_side = 1 - side
     near_hops = list(range(1, near))
@@ -340,27 +344,18 @@
     held_lanes = 2 * frames * width
     own_rows = pl.ds(pl.multiple_of(me * rows, SUBLANES), rows)
 
-    loads = []
-
-    def load(source, target):
-        loads.append(pltpu.make_async_copy(source, target, load_sem.at[len(loads)]))
-        loads[-1].start()
-
+    announce(peers)
     for coil in range(all_coils):
-        load(sens_ref.at[:, coil, :], sens_v.at[coil])
+        pltpu.make_async_copy(sens_ref.at[:, coil, :], sens_v.at[coil], load_sem.at[0]).start()
     for frame in range(frames):
-        load(image_ref.at[:, frame, :], image_v.at[frame])
-    load(rows_ref, rows_v)
-    load(cols_ref, cols_v)
-
-    def data_copy(pair, odd):
-        return pltpu.make_async_copy(
-            kspace_ref.at[:, odd, pair, :], data_ref.at[pair, odd], data_sem.at[pair, odd]
-        )
-
+        pltpu.make_async_copy(image_ref.at[:, frame, :], image_v.at[frame], load_sem.at[1]).start()
+    pltpu.make_async_copy(rows_ref, rows_v, load_sem.at[2]).start()
+    pltpu.make_async_copy(cols_ref, cols_v, load_sem.at[3]).start()
     for pair in range(coils * frames):
         for odd in range(2):
-            data_copy(pair, odd).start()
+            pltpu.make_async_copy(
+                kspace_ref.at[:, odd, pair, :], data_ref.at[pair, odd], load_sem.at[4]
+            ).start()
 
     def remote(source, target, send, recv, peer):
         return pltpu.make_async_remote_copy(
@@ -377,8 +372,8 @@
         return remote(
             sens_ref.at[:, peer * coils + coil, :],
             maps_ref.at[coil, own_rows, :],
-            maps_send.at[hop - 1, coil],
-            maps_recv.at[hop - 1, coil],
+            maps_send.at[0],
+            maps_recv.at[hop // near],
             peer,
         )
 
@@ -391,8 +386,8 @@
         return remote(
             packed_ref.at[peer, :, lanes],
             landed_ref.at[me, :, lanes],
-            pack_send.at[hop - 1],
-            pack_recv.at[hop - 1],
+            pack_send.at[hop // near],
+            pack_recv.at[hop // near],
             peer,
         )
 
@@ -405,8 +400,8 @@
         return remote(
             relay_ref.at[peer % near],
             relay_part(side, me % near * coils, far_side),
-            relay_send.at[hop - 1],
-            relay_recv.at[hop - 1],
+            relay_send.at[0],
+            relay_recv.at[0],
             peer,
         )
 
@@ -421,7 +416,7 @@
         return remote(
             kept_part(stage, phase, frame, True),
             gots[stage].at[landing, frame],
-            sum_send.at[phase, frame, stage],
+            sum_send.at[stage],
             sum_recv.at[landing, frame, stage],
             me + (1 - 2 * own_bits[stage]) * (1 << stage),
         )
@@ -439,13 +434,13 @@
         else:
             sums[stage + 1][phase, frame] = total
 
-    greet(peers)
+    pl.semaphore_wait(pltpu.get_barrier_semaphore(), len(peers))
     early = near // 2
     for hop in near_hops + far_hops[:early]:
         for coil in range(coils):
             maps_copy(hop, coil).start()
-    for copy in loads:
-        copy.wait()
+    drain(sens_v, load_sem.at[0])
+    drain(image_v, load_sem.at[1])
     pack_kernel(devices, width, sens_v, image_v, packed_ref)
     for at in range(near - 1):
         if at < early:
@@ -466,9 +461,9 @@
         mask_ref[...].astype(jnp.float32).astype(jnp.bfloat16),
         jnp.where(picked, 1.0, 0.0).astype(jnp.bfloat16),
     )
-    for pair in range(coils * frames):
-        for odd in range(2):
-            data_copy(pair, odd).wait()
+    drain(rows_v, load_sem.at[2])
+    drain(cols_v, load_sem.at[3])
+    drain(data_ref, load_sem.at[4])
 
     def transform(frame):
         mixes = []
@@ -533,9 +528,7 @@
 
         @pl.when(frame == lead)
         def wait_near():
-            for hop in near_hops:
-                for coil in range(coils):
-                    maps_copy(hop, coil).wait_recv()
+            drain(maps_ref.at[:, pl.ds(0, (near - 1) * rows), :], maps_recv.at[0])
 
         @pl.when(frame >= lead)
         def offer_near():
@@ -555,14 +548,12 @@
     for hop in far_hops:
         if hop // 2 % 2:
             pack_copy(hop).start()
-    for hop in far_hops:
-        for coil in range(coils):
-            maps_copy(hop, coil).wait_recv()
-
-    def project(frame):
+    drain(maps_ref.at[:, pl.ds(0, near * rows), :], maps_recv.at[1])
+
+    def project(sweep, frame):
         shape = (all_coils, width, length)
         maps_re, maps_im = (own_ref[:, 0].reshape(shape), own_ref[:, 1].reshape(shape))
-        now_re, now_im = (now_ref[0, frame][None], now_ref[1, frame][None])
+        now_re, now_im = (now_ref[sweep, 0, frame][None], now_ref[sweep, 1, frame][None])
         seen_re = (maps_re * now_re - maps_im * now_im).reshape(all_coils * width, length)
         seen_im = (maps_re * now_im + maps_im * now_re).reshape(all_coils * width, length)
         parts = []
@@ -575,8 +566,8 @@
         near, far = (parts[0] + parts[1], parts[0] - parts[1])
         kept_re = jnp.concatenate([near[:, :low], far[:, :low]], 1).reshape(shape)
         kept_im = jnp.concatenate([near[:, low:], far[:, low:]], 1).reshape(shape)
-        grad_ref[0, frame] = jnp.sum(maps_re * kept_re + maps_im * kept_im, 0)
-        grad_ref[1, frame] = jnp.sum(maps_re * kept_im - maps_im * kept_re, 0)
+        grad_ref[sweep, 0, frame] = jnp.sum(maps_re * kept_re + maps_im * kept_im, 0)
+        grad_ref[sweep, 1, frame] = jnp.sum(maps_re * kept_im - maps_im * kept_re, 0)
 
     def turn_maps():
         lines = pl.ds(pl.multiple_of(far_side * low, LANES), low)
@@ -595,13 +586,12 @@
         target[..., rows_at] = turned.reshape(target.shape[:-1] + (low,))
 
     def take_columns():
-        for hop in range(1, devices):
-            pack_copy(hop).wait_recv()
-        for hop in near_hops:
-            relay_copy(hop).wait_recv()
+        drain(landed_ref.at[pl.ds(0, near - 1)], pack_recv.at[0])
+        drain(landed_ref.at[pl.ds(0, near), :, pl.ds(0, block + held_lanes)], pack_recv.at[1])
+        drain(relay_ref.at[pl.ds(0, near - 1)], relay_recv.at[0])
         for row_side in (side, far_side):
             lines = pl.ds(row_side * near, near)
-            unfold(now_ref, row_side, lines, pl.ds(block, held_lanes))
+            unfold(now_ref.at[0], row_side, lines, pl.ds(block, held_lanes))
         for coil_side, row_side in ((0, side), (1, side), (far_side, far_side)):
             start = pl.multiple_of(coil_side * (block + held_lanes), LANES)
             lines = pl.ds(row_side * near, near)
@@ -612,74 +602,97 @@
         if turn == 0:
             turn_maps()
         pass_on(1, 0, turn)
-    for stage in range(2, bits - 2):
-        for turn in range(frames):
-            pass_on(stage - 1, 1, turn)
-            pass_on(stage, 0, turn)
-    first = min(1, frames - 1)
-    for turn in range(frames + 2):
-        if turn < frames:
-            pass_on(bits - 3, 1, turn)
-            pass_on(bits - 2, 0, turn)
-        pass_on(bits - 2, 1, turn - 2)
-        if turn == first:
-            take_columns()
-        if first <= turn < frames:
-            project(turn - first)
-    for frame in range(frames - first, frames):
-        project(frame)
-    for phase in range(2):
-        for frame in range(frames):
-            collect(bits - 1, phase, frame)
-
-    for sweep in range(OUTER):
-        if sweep:
-            for frame in range(frames):
-                project(frame)
-        for part in range(2):
-            target = []
-            for frame in range(frames):
-                data_term = total_ref[frame, part * width : (part + 1) * width]
-                gradient = grad_ref[part, frame] - data_term
-                target.append(now_ref[part, frame] - step_size * gradient)
-            for frame, value in enumerate(denoise_frames(target)):
-                now_ref[part, frame] = value
-
-    turned = jnp.transpose(now_ref[...].reshape(2 * frames * width, length))
-    ready_ref[...] = turned.reshape(ready_ref.shape)
-
-    def back_copy(hop):
+    projected = [0] * OUTER
+    settled = [0] * OUTER
+    summed = [0]
+
+    def project_to(sweep, count):
+        while projected[sweep] < min(count, frames):
+            if sweep and projected[sweep] == settled[sweep - 1]:
+                advance(sweep - 1)
+            project(sweep, projected[sweep])
+            projected[sweep] += 1
+
+    def back_copy(piece, hop):
         peer = peers[hop - 1]
         return remote(
-            ready_ref.at[peer], back_ref.at[me], back_send.at[hop - 1], back_recv.at[hop - 1], peer
+            ready_ref.at[piece, peer],
+            back_ref.at[piece, me],
+            back_send.at[piece],
+            back_recv.at[piece],
+            peer,
         )
 
-    for hop in range(1, devices):
-        back_copy(hop).start()
-    back_ref[me] = ready_ref[me]
-    for hop in range(1, devices):
-        back_copy(hop).wait_recv()
-    for part in range(2):
+    def settle(sweep, part, start, stop):
+        first = max(0, start - INNER)
+        target = []
+        for frame in range(first, min(frames, stop + INNER)):
+            data_term = total_ref[frame, part * width : (part + 1) * width]
+            gradient = grad_ref[sweep, part, frame] - data_term
+            target.append(now_ref[sweep, part, frame] - step_size * gradient)
+        return denoise_frames(target)[start - first : stop - first]
+
+    def advance(sweep):
+        start = settled[sweep]
+        stop = start + (some if sweep == OUTER - 1 else max(1, some // 2))
+        project_to(sweep, stop + INNER)
+        while summed[0] < min(frames, stop + INNER):
+            for phase in range(2):
+                collect(bits - 1, phase, summed[0])
+            summed[0] += 1
+        parts = [settle(sweep, part, start, stop) for part in range(2)]
+        settled[sweep] = stop
+        if sweep < OUTER - 1:
+            for part in range(2):
+                for frame, value in enumerate(parts[part]):
+                    now_ref[sweep + 1, part, start + frame] = value
+            return
+        piece = start // some
+        turned = jnp.transpose(jnp.concatenate(parts[0] + parts[1], 0))
+        ready_ref[piece] = turned.reshape(ready_ref.shape[1:])
+        for hop in far_hops + near_hops:
+            back_copy(piece, hop).start()
+        back_ref[piece, me] = ready_ref[piece, me]
+
+    for turn in range(frames):
+        pass_on(1, 1, turn)
+        pass_on(2, 0, turn)
+        pass_on(2, 1, turn - 2)
+        if turn == 1:
+            take_columns()
+        project_to(0, turn)
+
+    for frame in range(frames - 2, frames):
+        if bits == 4:
+            project_to(1, frame + 3 - frames)
+        pass_on(2, 1, frame)
+    for stage in range(3, bits - 1):
+        for phase in range(2):
+            for frame in range(frames):
+                pass_on(stage, phase, frame)
+
+    for piece in range(2):
+        advance(OUTER - 1)
+    for piece in range(2):
+        drain(back_ref.at[piece, pl.ds(0, devices - 1)], back_recv.at[piece])
         for first in range(0, frames, group):
-            lane = (part * frames + first) * width
             for tile in range(devices // group):
                 taken = [
-                    back_ref[tile * group + at, :, lane : lane + LANES] for at in range(group)
+                    back_ref[piece, tile * group + at, :, first * width : first * width + LANES]
+                    for at in range(group)
                 ]
-                target = part * half + tile * LANES
                 for at, value in enumerate(swap_blocks(taken, width)):
-                    out_ref[:, first + at, target : target + LANES] = value
-    for hop in range(1, devices):
-        for coil in range(coils):
-            maps_copy(hop, coil).wait_send()
-        pack_copy(hop).wait_send()
-        if hop < near:
-            relay_copy(hop).wait_send()
-        back_copy(hop).wait_send()
-    for frame in range(frames):
-        for stage in range(bits):
-            for phase in range(2):
-                sum_copy(stage, phase, frame).wait_send()
+                    part, frame = ((first + at) // some, piece * some + (first + at) % some)
+                    target = part * half + tile * LANES
+                    out_ref[:, frame, target : target + LANES] = value
+    drain(maps_ref.at[:, pl.ds(0, (devices - 1) * rows), :], maps_send.at[0])
+    drain(landed_ref.at[pl.ds(0, near - 1)], pack_send.at[0])
+    drain(landed_ref.at[pl.ds(0, near), :, pl.ds(0, block + held_lanes)], pack_send.at[1])
+    drain(relay_ref.at[pl.ds(0, near - 1)], relay_send.at[0])
+    for piece in range(2):
+        drain(back_ref.at[piece, pl.ds(0, devices - 1)], back_send.at[piece])
+    for stage in range(bits):
+        drain(gots[stage], sum_send.at[stage])
 
 
 def reconstruct(image, sens, kspace, mask, devices):
@@ -719,27 +732,26 @@
             held(devices, rows, lanes),
             held(devices, rows, lanes),
             held(2, 2, all_coils // 2, width, length),
-            held(2, frames, width, length),
-            held(2, frames, width, length),
+            held(OUTER, 2, frames, width, length),
+            held(OUTER, 2, frames, width, length),
             pltpu.VMEM((frames, 2, 2, length, length), jnp.bfloat16),
             held(devices // 2, 2, coils, width, length // 2),
             held(frames, 2 * width, length),
-            held(devices, rows, 2 * frames * width),
-            held(devices, rows, 2 * frames * width),
+            held(2, devices, rows, frames * width),
+            held(2, devices, rows, frames * width),
             *sums,
             *gots,
-            dma((all_coils + frames + 2,)),
-            dma((pairs, 2)),
-            dma((devices - 1, coils)),
-            dma((devices - 1, coils)),
-            dma((devices - 1,)),
-            dma((devices - 1,)),
-            dma((devices // 2 - 1,)),
-            dma((devices // 2 - 1,)),
+            dma((5,)),
+            dma((1,)),
+            dma((2,)),
+            dma((2,)),
+            dma((2,)),
+            dma((1,)),
+            dma((1,)),
+            dma((bits,)),
             dma((2, frames, bits)),
-            dma((2, frames, bits)),
-            dma((devices - 1,)),
-            dma((devices - 1,)),
+            dma((2,)),
+            dma((2,)),
         ],
         compiler_params=pltpu.CompilerParams(
             collective_id=0, has_side_effects=True, vmem_limit_bytes=60 * 1024 * 1024

time: 84.3 us -> 77.9 us (0.924)
  Pallas kernels: 82.4 us -> 76.1 us
    pallas_call x1, Pallas kernels: 82.4 us -> 76.1 us  [reconstruct(): pl.pallas_call(lambda *refs: whole_kernel(devices, *refs), out_shape=jax....]
where the time goes in v3:
time: 77.9 us; the launch traced here: 77.8 us
  Pallas kernels  76.1 us (98%)
  local copies, waits for them, and re-layouts  1.67 us (2%)
    pallas_call x1, Pallas kernels, reconstruct(): pl.pallas_call(lambda *refs: whole_kernel(devices, *refs), out_shape=jax....  76.1 us
    unnamed x1, local copies, waits for them, and re-layouts  1.67 us

profile of v3, /device:TPU:0, one launch (start us, length us, event | category | flops | bytes accessed | tf_op | source)
XLA Modules:
  0.0 77.8 jit_solution(6574825537630744265)
XLA Ops:
  0.0 76.1 %reconstruct.1 = f32[16,8,512]{2,1,0:T(8,128)} custom-call(f32[16,8,512]{2,1,0:T(8,128)} %refs_0_.1, f32[16,32,512]{2,1,0:T(8,128)} %refs_1_.1, f32[128,2,16,512]{3,2,1,0:T(8,128)} %bitcast.1, s32[8,256]{1,0:T(8,128)} %refs_3_.1, bf16[2,2,256,256]{3,2,1,0:T(8,128)(2,1)} %constant.4.clone.refs_4_, bf16[2,512,512]{2,1,0:T(8,128)(2,1)} %constant.5.clone.refs_5_), custom_call_target="tpu_custom_call" | custom-call | tf_op jit(solution)/shard_map/reconstruct/pallas_call | solution.py:718
  76.1 1.7 %copy.8 = f32[16,8,512]{2,1,0:T(8,128)} copy(f32[16,8,512]{2,1,0:T(8,128)} %reconstruct.1) | data formatting | bytes 524288

commit v4 on v3

--- a/solution.py
+++ b/solution.py
@@ -249,32 +249,6 @@
 
 def clipped(value):
     return jnp.minimum(jnp.maximum(value, -1.0), 1.0)
-
-
-def denoise_frames(target):
-    frames = len(target)
-    dual_time = [None] * frames
-    dual_rows = [None] * frames
-
-    def lowered(frame):
-        moved = spread_rows(dual_rows[frame])
-        if frame > 0:
-            moved = moved + dual_time[frame - 1]
-        if frame < frames - 1:
-            moved = moved - dual_time[frame]
-        return target[frame] - tv_weight * moved
-
-    primal = target
-    for repeat in range(INNER):
-        if repeat:
-            primal = [lowered(frame) for frame in range(frames)]
-        for frame in range(frames):
-            rows = dual_step * row_steps(primal[frame])
-            dual_rows[frame] = clipped(rows if not repeat else dual_rows[frame] + rows)
-            if frame < frames - 1:
-                time = dual_step * (primal[frame + 1] - primal[frame])
-                dual_time[frame] = clipped(time if not repeat else dual_time[frame] + time)
-    return [lowered(frame) for frame in range(frames)]
 
 
 def whole_kernel(
@@ -330,9 +304,13 @@
     group = LANES // width
     me = lax.axis_index("coil")
     own_bits = [me // (1 << bit) % 2 for bit in range(bits)]
+    inner = (own_bits[bits - 1] + own_bits[bits - 2]) % 2
     peers = []
     for hop in range(1, devices):
-        flips = [(own_bits[bit] + (hop >> bit)) % 2 * (1 << bit) for bit in range(bits)]
+        turns = [hop >> bit for bit in range(bits)]
+        if hop >= devices // 2:
+            turns[bits - 2] += inner
+        flips = [(own_bits[bit] + turns[bit]) % 2 * (1 << bit) for bit in range(bits)]
         peers.append(sum(flips[1:], flips[0]))
     near = devices // 2
     some = frames // 2
@@ -521,7 +499,7 @@
             sum_copy(0, phase, frame).start()
         pass_on(0, phase, frame - 1)
 
-    lead = min(3, frames - 1)
+    lead = min(1, frames - 1)
 
     def step(frame, unused):
         transform(frame)
@@ -603,15 +581,71 @@
             turn_maps()
         pass_on(1, 0, turn)
     projected = [0] * OUTER
-    settled = [0] * OUTER
     summed = [0]
+    known = {}
 
     def project_to(sweep, count):
         while projected[sweep] < min(count, frames):
-            if sweep and projected[sweep] == settled[sweep - 1]:
-                advance(sweep - 1)
-            project(sweep, projected[sweep])
+            frame = projected[sweep]
+            if sweep:
+                for part in range(2):
+                    now_ref[sweep, part, frame] = primal(sweep - 1, part, INNER, frame)
+            if sweep:
+                prepare(sweep - 1, frame + INNER)
+            project(sweep, frame)
             projected[sweep] += 1
+            if sweep == OUTER - 1:
+                prepare(sweep, frame)
+
+    def target_of(sweep, part, frame):
+        project_to(sweep, frame + 1)
+        while summed[0] <= frame:
+            for phase in range(2):
+                collect(bits - 1, phase, summed[0])
+            summed[0] += 1
+        data_term = total_ref[frame, part * width : (part + 1) * width]
+        gradient = grad_ref[sweep, part, frame] - data_term
+        return now_ref[sweep, part, frame] - step_size * gradient
+
+    def dual_time(sweep, part, count, frame):
+        ahead = primal(sweep, part, count - 1, frame + 1)
+        steps = dual_step * (ahead - primal(sweep, part, count - 1, frame))
+        if count > 1:
+            steps = recall(dual_time, sweep, part, count - 1, frame) + steps
+        return clipped(steps)
+
+    def dual_rows(sweep, part, count, frame):
+        steps = dual_step * row_steps(primal(sweep, part, count - 1, frame))
+        if count > 1:
+            steps = recall(dual_rows, sweep, part, count - 1, frame) + steps
+        return clipped(steps)
+
+    def rows_apart(sweep, part, count, frame):
+        return spread_rows(recall(dual_rows, sweep, part, count, frame))
+
+    def prepare(sweep, newest):
+        for count in range(1, INNER + 1):
+            if 0 <= newest - count + 1 < frames:
+                for part in range(2):
+                    recall(rows_apart, sweep, part, count, newest - count + 1)
+
+    def lowered(sweep, part, count, frame):
+        moved = recall(rows_apart, sweep, part, count, frame)
+        if frame > 0:
+            moved = moved + recall(dual_time, sweep, part, count, frame - 1)
+        if frame < frames - 1:
+            moved = moved - recall(dual_time, sweep, part, count, frame)
+        return recall(target_of, sweep, part, frame) - tv_weight * moved
+
+    def recall(rule, *where):
+        if (rule, where) not in known:
+            known[rule, where] = rule(*where)
+        return known[rule, where]
+
+    def primal(sweep, part, count, frame):
+        if count:
+            return recall(lowered, sweep, part, count, frame)
+        return recall(target_of, sweep, part, frame)
 
     def back_copy(piece, hop):
         peer = peers[hop - 1]
@@ -623,44 +657,14 @@
             peer,
         )
 
-    def settle(sweep, part, start, stop):
-        first = max(0, start - INNER)
-        target = []
-        for frame in range(first, min(frames, stop + INNER)):
-            data_term = total_ref[frame, part * width : (part + 1) * width]
-            gradient = grad_ref[sweep, part, frame] - data_term
-            target.append(now_ref[sweep, part, frame] - step_size * gradient)
-        return denoise_frames(target)[start - first : stop - first]
-
-    def advance(sweep):
-        start = settled[sweep]
-        stop = start + (some if sweep == OUTER - 1 else max(1, some // 2))
-        project_to(sweep, stop + INNER)
-        while summed[0] < min(frames, stop + INNER):
-            for phase in range(2):
-                collect(bits - 1, phase, summed[0])
-            summed[0] += 1
-        parts = [settle(sweep, part, start, stop) for part in range(2)]
-        settled[sweep] = stop
-        if sweep < OUTER - 1:
-            for part in range(2):
-                for frame, value in enumerate(parts[part]):
-                    now_ref[sweep + 1, part, start + frame] = value
-            return
-        piece = start // some
-        turned = jnp.transpose(jnp.concatenate(parts[0] + parts[1], 0))
-        ready_ref[piece] = turned.reshape(ready_ref.shape[1:])
-        for hop in far_hops + near_hops:
-            back_copy(piece, hop).start()
-        back_ref[piece, me] = ready_ref[piece, me]
-
     for turn in range(frames):
         pass_on(1, 1, turn)
         pass_on(2, 0, turn)
         pass_on(2, 1, turn - 2)
         if turn == 1:
             take_columns()
-        project_to(0, turn)
+        if turn:
+            project_to(0, (turn * frames + 2) // 5)
 
     for frame in range(frames - 2, frames):
         if bits == 4:
@@ -672,7 +676,15 @@
                 pass_on(stage, phase, frame)
 
     for piece in range(2):
-        advance(OUTER - 1)
+        settled = []
+        for frame in range(piece * some, (piece + 1) * some):
+            settled.append([primal(OUTER - 1, part, INNER, frame) for part in range(2)])
+        settled = [pair[0] for pair in settled] + [pair[1] for pair in settled]
+        turned = jnp.transpose(jnp.concatenate(settled, 0))
+        ready_ref[piece] = turned.reshape(ready_ref.shape[1:])
+        for hop in far_hops[::-1] + near_hops[::-1]:
+            back_copy(piece, hop).start()
+        back_ref[piece, me] = ready_ref[piece, me]
     for piece in range(2):
         drain(back_ref.at[piece, pl.ds(0, devices - 1)], back_recv.at[piece])
         for first in range(0, frames, group):

time: 77.9 us -> 76 us (0.976)
  Pallas kernels: 76.1 us -> 74.1 us
    pallas_call x1, Pallas kernels: 76.1 us -> 74.1 us  [reconstruct(): pl.pallas_call(lambda *refs: whole_kernel(devices, *refs), out_shape=jax....]
where the time goes in v4:
time: 76 us; the launch traced here: 75.8 us
  Pallas kernels  74.1 us (97%)
  local copies, waits for them, and re-layouts  1.67 us (2%)
    pallas_call x1, Pallas kernels, reconstruct(): pl.pallas_call(lambda *refs: whole_kernel(devices, *refs), out_shape=jax....  74.1 us
    unnamed x1, local copies, waits for them, and re-layouts  1.67 us

profile of v4, /device:TPU:0, one launch (start us, length us, event | category | flops | bytes accessed | tf_op | source)
XLA Modules:
  0.0 75.8 jit_solution(16312261338661065768)
XLA Ops:
  0.0 74.1 %reconstruct.1 = f32[16,8,512]{2,1,0:T(8,128)} custom-call(f32[16,8,512]{2,1,0:T(8,128)} %refs_0_.1, f32[16,32,512]{2,1,0:T(8,128)} %refs_1_.1, f32[128,2,16,512]{3,2,1,0:T(8,128)} %bitcast.1, s32[8,256]{1,0:T(8,128)} %refs_3_.1, bf16[2,2,256,256]{3,2,1,0:T(8,128)(2,1)} %constant.4.clone.refs_4_, bf16[2,512,512]{2,1,0:T(8,128)(2,1)} %constant.5.clone.refs_5_), custom_call_target="tpu_custom_call" | custom-call | tf_op jit(solution)/shard_map/reconstruct/pallas_call | solution.py:730
  74.1 1.7 %copy.8 = f32[16,8,512]{2,1,0:T(8,128)} copy(f32[16,8,512]{2,1,0:T(8,128)} %reconstruct.1) | data formatting | bytes 524288

commit v5 on v4

--- a/solution.py
+++ b/solution.py
@@ -576,9 +576,9 @@
             unfold(own_ref.at[coil_side], row_side, lines, pl.ds(start, block))
 
     for turn in range(frames + 1):
-        offer(1, turn)
         if turn == 0:
             turn_maps()
+        offer(1, turn)
         pass_on(1, 0, turn)
     projected = [0] * OUTER
     summed = [0]
@@ -660,6 +660,8 @@
     for turn in range(frames):
         pass_on(1, 1, turn)
         pass_on(2, 0, turn)
+        if bits == 4 and turn == frames - 1:
+            project_to(1, 1)
         pass_on(2, 1, turn - 2)
         if turn == 1:
             take_columns()
@@ -668,7 +670,7 @@
 
     for frame in range(frames - 2, frames):
         if bits == 4:
-            project_to(1, frame + 3 - frames)
+            project_to(1, frame + 4 - frames)
         pass_on(2, 1, frame)
     for stage in range(3, bits - 1):
         for phase in range(2):

time: 76 us -> 75.9 us (level)
  no operation moved by 1% of the time
where the time goes in v5:
time: 75.9 us; the launch traced here: 75.7 us
  Pallas kernels  74.1 us (98%)
  local copies, waits for them, and re-layouts  1.67 us (2%)
    pallas_call x1, Pallas kernels, reconstruct(): pl.pallas_call(lambda *refs: whole_kernel(devices, *refs), out_shape=jax....  74.1 us
    unnamed x1, local copies, waits for them, and re-layouts  1.67 us

profile of v5, /device:TPU:0, one launch (start us, length us, event | category | flops | bytes accessed | tf_op | source)
XLA Modules:
  0.0 75.7 jit_solution(5555026349532017871)
XLA Ops:
  0.0 74.1 %reconstruct.1 = f32[16,8,512]{2,1,0:T(8,128)} custom-call(f32[16,8,512]{2,1,0:T(8,128)} %refs_0_.1, f32[16,32,512]{2,1,0:T(8,128)} %refs_1_.1, f32[128,2,16,512]{3,2,1,0:T(8,128)} %bitcast.1, s32[8,256]{1,0:T(8,128)} %refs_3_.1, bf16[2,2,256,256]{3,2,1,0:T(8,128)(2,1)} %constant.4.clone.refs_4_, bf16[2,512,512]{2,1,0:T(8,128)(2,1)} %constant.5.clone.refs_5_), custom_call_target="tpu_custom_call" | custom-call | tf_op jit(solution)/shard_map/reconstruct/pallas_call | solution.py:732
  74.1 1.7 %copy.8 = f32[16,8,512]{2,1,0:T(8,128)} copy(f32[16,8,512]{2,1,0:T(8,128)} %reconstruct.1) | data formatting | bytes 524288
